TPU v7x, 256 devices: a whole 4x4x8 slice. The times are simulated.
256 devices in a mesh: req: 8 (over z_lo, y), dev: 32 (over z_hi, x, core).
Axes of the slice: x: 4, y: 4, z: 8 (z_hi: 4, z_lo: 2; z = z_hi * 2 + z_lo), core: 2. Of those that a mesh axis runs over, the one named last changes fastest.
Arguments:
- hidden_in: bfloat16 [8, 1024, 2048], P('req', 'dev'), may hold values from -60 to 60
- attention_gain: float32 [2048], replicated, may hold values from 0.1 to 1.9
- query_weight: bfloat16 [2048, 2048], P('dev'), may hold values from -0.625 to 0.625
- keyval_weight: bfloat16 [1024, 2048], P('dev'), may hold values from -0.5 to 0.5
- out_weight: bfloat16 [2048, 2048], P('dev'), may hold values from -0.0625 to 0.0625
- feedforward_gain: float32 [2048], replicated, may hold values from 0.1 to 1.9
- gate_weight: bfloat16 [8192, 2048], P(('req', 'dev')), may hold values from -0.125 to 0.125
- up_weight: bfloat16 [8192, 2048], P(('req', 'dev')), may hold values from -0.125 to 0.125
- down_weight: bfloat16 [8192, 2048], P(('req', 'dev')), may hold values from -0.0625 to 0.0625
- prefix_pool: bfloat16 [8, 256, 16, 8, 128], P('req', 'dev'), may hold values from -640 to 640
- page_table: int32 [8, 256], P('req'), may hold values from 0 to 255, each once within a row
- prefix_length: int32 [8], P('req'), may hold values from 1 to 4096, 20480 in all
Outputs:
- hidden_out: bfloat16 [8, 1024, 2048], P('req', 'dev')
- new_keyval: bfloat16 [8, 1024, 8, 128], P('req', 'dev')
Inputs may be any that keep to these rules, and one draw needn't show every extreme that they name: `page_table`: each row names every page of the request's pool once. `prefix_length`: the longest cached prefix is exactly 4096.
All inputs are finite; a program needn't handle non-finite values. No bound on the sum of `prefix_length` on one device may be relied on, other than what follows from the above.
Results may differ from a plain program's by a relative error of at most 0.013.
The roundings to bfloat16 on the way count: a program that leaves them out, or rounds other values in their place, can miss the bound.
Values may be sent and summed in bfloat16 or wider, within the bound.
A program may use at most 64 MiB of HBM per device.

v0:
```python
import jax
import jax.numpy as jnp
from jax import lax
from jax.sharding import PartitionSpec as P

HQ = 32
KVH = 8
HD = 64
PAGE = 16
KBLOCK = 512
ROPE_BASE = 10000000.0
EPS = 1e-05
ATTENTION_SCALE = 0.015625
MASKED = -1e30


def root_norm(activations, norm_gain):
    widened = activations.astype(jnp.float32)
    inverse_rms = lax.rsqrt(jnp.mean(widened * widened, axis=-1, keepdims=True) + EPS)
    return (widened * inverse_rms * norm_gain).astype(jnp.bfloat16)


def rotate(vector, positions):
    half_width = vector.shape[-1] // 2
    frequency = ROPE_BASE ** (-jnp.arange(half_width, dtype=jnp.float32) / half_width)
    angles = positions.astype(jnp.float32)[:, None] * frequency[None, :]
    cosine = jnp.cos(angles)[:, None, :]
    sine_part = jnp.sin(angles)[:, None, :]
    leading = vector[..., :half_width]
    trailing = vector[..., half_width:]
    return jnp.concatenate(
        [leading * cosine - trailing * sine_part, trailing * cosine + leading * sine_part], axis=-1
    )


def transposed_product(left, right):
    return lax.dot_general(
        left, right, (((1,), (1,)), ((), ())), preferred_element_type=jnp.float32
    )


def attend_block(carried, queries, key_part, value_part, allowed):
    row_max, row_total, summed = carried
    scores = transposed_product(queries, key_part)
    scores = jnp.where(allowed, scores, MASKED)
    new_max = jnp.maximum(row_max, jnp.max(scores, axis=1))
    factor = jnp.exp(row_max - new_max)
    weights = jnp.where(allowed, jnp.exp(scores - new_max[:, None]), 0.0)
    new_total = row_total * factor + jnp.sum(weights, axis=1)
    summed = summed * factor[:, None] + jnp.dot(
        weights.astype(jnp.bfloat16), value_part, preferred_element_type=jnp.float32
    )
    return (new_max, new_total, summed)


def on_device(
    hidden_in,
    attention_gain,
    query_weight,
    keyval_weight,
    out_weight,
    feedforward_gain,
    gate_weight,
    up_weight,
    down_weight,
    prefix_pool,
    page_table,
    prefix_length,
):
    local_tokens = hidden_in.shape[1]
    device_count = lax.axis_size("dev")
    all_count = local_tokens * device_count
    heads_here = query_weight.shape[0] // HD
    group_size = HQ // KVH
    member = lax.axis_index("dev")
    length = prefix_length[0]
    own_tokens = hidden_in[0]
    all_tokens = lax.all_gather(own_tokens, "dev", axis=0, tiled=True)
    normed = root_norm(all_tokens, attention_gain)
    positions = length + jnp.arange(all_count, dtype=jnp.int32)
    raw_columns = transposed_product(keyval_weight, normed).astype(jnp.bfloat16)
    keyval_all = lax.all_gather(raw_columns, "dev", axis=0, tiled=True)
    own_rows = lax.dynamic_slice_in_dim(
        keyval_all, member * local_tokens, local_tokens, 1
    ).T.reshape(local_tokens, KVH, 2 * HD)
    own_positions = lax.dynamic_slice_in_dim(positions, member * local_tokens, local_tokens, 0)
    own_keys = rotate(own_rows[..., :HD].astype(jnp.float32), own_positions).astype(jnp.bfloat16)
    new_keyval = jnp.concatenate([own_keys, own_rows[..., HD:]], axis=-1)
    shared_head = member * heads_here // group_size
    head_pair = lax.dynamic_slice_in_dim(keyval_all, shared_head * 2 * HD, 2 * HD, 0).T
    fresh_keys = rotate(head_pair[:, None, :HD].astype(jnp.float32), positions)[:, 0, :].astype(
        jnp.bfloat16
    )
    fresh_values = head_pair[:, HD:]
    query_full = transposed_product(normed, query_weight).reshape(all_count, heads_here, HD)
    queries = (
        (rotate(query_full, positions) * ATTENTION_SCALE)
        .astype(jnp.bfloat16)
        .reshape(all_count * heads_here, HD)
    )
    local_pool = prefix_pool[0]
    wanted = jnp.arange(device_count, dtype=jnp.int32) * heads_here // group_size
    outgoing = jnp.take(local_pool, wanted, axis=2)
    incoming = lax.all_to_all(outgoing, "dev", split_axis=2, concat_axis=0, tiled=True)
    pool_head = incoming[:, :, 0, :]
    page_rows = page_table[0]
    block_pages = KBLOCK // PAGE
    query_rows = all_count * heads_here
    carried = (
        jnp.full((query_rows,), MASKED, jnp.float32),
        jnp.zeros((query_rows,), jnp.float32),
        jnp.zeros((query_rows, HD), jnp.float32),
    )

    def prefix_step(block_index, running):
        page_ids = lax.dynamic_slice_in_dim(page_rows, block_index * block_pages, block_pages, 0)
        stored = jnp.take(pool_head, page_ids, axis=0).reshape(KBLOCK, 2 * HD)
        slot_ids = block_index * KBLOCK + jnp.arange(KBLOCK, dtype=jnp.int32)
        allowed = (slot_ids < length)[None, :]
        return attend_block(running, queries, stored[:, :HD], stored[:, HD:], allowed)

    block_count = (length + KBLOCK - 1) // KBLOCK
    carried = lax.fori_loop(0, block_count, prefix_step, carried)
    query_token = jnp.arange(query_rows, dtype=jnp.int32) // heads_here
    causal = jnp.arange(all_count, dtype=jnp.int32)[None, :] <= query_token[:, None]
    row_max, row_total, summed = attend_block(carried, queries, fresh_keys, fresh_values, causal)
    attended = (summed / row_total[:, None]).astype(jnp.bfloat16)
    rows_in = attended
    attention_own = lax.psum_scatter(
        jnp.dot(rows_in, out_weight, preferred_element_type=jnp.float32).astype(jnp.bfloat16),
        "dev",
        scatter_dimension=0,
        tiled=True,
    ).astype(jnp.float32)
    residual = own_tokens.astype(jnp.float32) + attention_own
    mlp_rows = lax.all_gather(root_norm(residual, feedforward_gain), "dev", axis=0, tiled=True)
    fetched = (
        lax.all_gather(gate_weight, "req", axis=0, tiled=True),
        lax.all_gather(up_weight, "req", axis=0, tiled=True),
        lax.all_gather(down_weight, "req", axis=0, tiled=True),
    )
    gate_rows, up_rows, down_rows = fetched
    rows_in = mlp_rows
    gate_act = transposed_product(rows_in, gate_rows)
    up_act = transposed_product(rows_in, up_rows)
    activated = (jax.nn.silu(gate_act) * up_act).astype(jnp.bfloat16)
    feedforward_own = lax.psum_scatter(
        jnp.dot(activated, down_rows, preferred_element_type=jnp.float32).astype(jnp.bfloat16),
        "dev",
        scatter_dimension=0,
        tiled=True,
    ).astype(jnp.float32)
    hidden_out = (residual + feedforward_own).astype(jnp.bfloat16)
    return (hidden_out[None], new_keyval[None])


def solution(mesh):
    placed = (
        P("req", "dev", None),
        P(),
        P("dev", None),
        P("dev", None),
        P("dev", None),
        P(),
        P(("req", "dev"), None),
        P(("req", "dev"), None),
        P(("req", "dev"), None),
        P("req", "dev", None, None, None),
        P("req", None),
        P("req"),
    )
    return jax.shard_map(
        on_device,
        mesh=mesh,
        in_specs=placed,
        out_specs=(P("req", "dev", None), P("req", "dev", None, None)),
        check_vma=False,
    )
```

profile of v0, /device:TPU:8, one launch (start us, length us, event | category | flops | bytes accessed | tf_op | source)
XLA Modules:
  0.0 542.3 jit_solution(16338885161745345462)
XLA Ops:
  8.1 0.7 all-gather.18.cloned.1.call-update
  8.8 65.8 %all-gather.18.cloned.1.call-done = bf16[1,1024,2048]{2,1,0:T(8,128)(2,1)} async-done(((bf16[1,32,2048]{2,1,0:T(8,128)(2,1)}), bf16[1,1024,2048]{2,1,0:T(8,128)(2,1)}) %all-gather.18.cloned.1.call-update) | async-done | bytes 4194320 | tf_op jit(solution)/shard_map/all_gather | solution.py:78
  74.6 3.2 fusion.11
  78.1 2.1 fusion.34
  80.2 0.8 gather_fusion.1
  81.1 1.1 select_bitcast_fusion
  82.2 6.6 %all-to-all-start = ((bf16[8,16,32,128]{3,1,0,2:T(8,128)(2,1)}), bf16[8,16,32,128]{3,1,0,2:T(8,128)(2,1)S(1)}, u32[]{:S(2)}, u32[]{:S(2)}) async-start(bf16[8,16,32,128]{3,1,0,2:T(8,128)(2,1)} %select_bitcast_fusion), calls=%async_computation | async-start | bytes 2097152 | tf_op jit(solution)/shard_map/all_to_all | solution.py:104
  89.6 3.7 fusion.25
  93.3 55.0 %all-gather.8.cloned.1.call-done = bf16[1024,1024]{1,0:T(8,128)(2,1)} async-done(((bf16[32,1024]{1,0:T(8,128)(2,1)}), bf16[1024,1024]{1,0:T(8,128)(2,1)}) %all-gather.8.cloned.1.call-update) | async-done | bytes 2097168 | tf_op jit(solution)/shard_map/all_gather | solution.py:82
  148.3 1.0 dynamic-slice_bitcast_fusion
  149.3 0.6 fusion.66
  150.2 13.3 %while.14 = (s32[]{:T(128)}, f32[1024]{0:T(1024)S(1)}, f32[1024]{0:T(1024)S(1)}, f32[1024,64]{0,1:T(8,128)S(1)}, s32[]{:T(128)}, /*index=5*/s32[]{:T(128)}, s32[...) while((s32[]{:T(128)}, f32[1024]{0:T(1024)S(1)}, ...), condition=%wide.region_4.5_spmd, body=%wide.region_1.4_spmd.sunk | while | flops 139661504 | bytes 7807763 | solution.py:123
  150.2 0.7 add_compare_fusion.2
  151.1 0.6 gather_fusion
  152.3 0.5 fusion.105
  152.8 0.6 convolution_add_fusion.2
  153.5 0.7 add_compare_fusion.2
  154.4 0.6 gather_fusion
  155.2 0.5 select_reduce_fusion.2
  155.7 0.5 fusion.105
  156.2 0.6 convolution_add_fusion.2
  156.9 0.7 add_compare_fusion.2
  157.8 0.6 gather_fusion
  159.0 0.5 fusion.105
  159.5 0.6 convolution_add_fusion.2
  160.2 0.7 add_compare_fusion.2
  161.1 0.6 gather_fusion
  161.8 0.5 select_reduce_fusion.2
  162.3 0.5 fusion.105
  162.8 0.6 convolution_add_fusion.2
  163.5 0.8 fusion.15
  164.3 2.0 copy-done.1
  166.7 5.8 %convolution_convert_fusion.1 = bf16[1024,2048]{1,0:T(8,128)(2,1)} fusion(bf16[64,2048]{1,0:T(8,128)(2,1)S(1)} %copy-done, f32[1024,1024]{0,1:T(8,128)} %copy-done.1, f32[1024]{0:T(1024)S(1)} %max.6, f32[1024,64]{0,1:T(8,128)S(1)} %get-tuple-element.52, bf16[1024,128]{0,1:T(8,128)(2,1)S(1)} %dynamic-slice_bitcast_fusion, f32[1024]{0:T(1024)S(1)} %get-tuple-element.95, ...), kind=kOutput, calls=%fused_computation.31 | convolution fusion | flops 410255360 | bytes 9056256 | tf_op jit(solution)/shard_map/dot_general | solution.py:130
  172.6 0.5 all-gather.12.cloned.1.call-update
  173.2 108.5 %reduce-scatter.3.cloned.1.call-done = bf16[32,2048]{1,0:T(8,128)(2,1)} async-done(((bf16[1024,2048]{1,0:T(8,128)(2,1)}), bf16[32,2048]{1,0:T(8,128)(2,1)}) %reduce-scatter.3.cloned.1.call-update) | async-done | bytes 131088 | tf_op jit(solution)/shard_map/reduce_scatter | solution.py:129
  281.7 1.1 multiply_reduce_fusion
  282.8 1.7 multiply_convert_fusion
  284.5 0.5 all-gather.14.cloned.1.call-update
  285.1 0.7 all-gather.16.cloned.1.call-update
  286.0 56.1 %all-gather.10.cloned.1.call-done = bf16[1024,2048]{1,0:T(8,128)(2,1)} async-done(((bf16[32,2048]{1,0:T(8,128)(2,1)}), bf16[1024,2048]{1,0:T(8,128)(2,1)}) %all-gather.10.cloned.1.call-update) | async-done | bytes 4194320 | tf_op jit(solution)/shard_map/all_gather | solution.py:136
  342.1 3.8 fusion.87
  345.9 34.9 %all-gather.14.cloned.1.call-done = bf16[256,2048]{1,0:T(8,128)(2,1)} async-done(((bf16[32,2048]{1,0:T(8,128)(2,1)}), bf16[256,2048]{1,0:T(8,128)(2,1)}) %all-gather.14.cloned.1.call-update) | async-done | bytes 1048592 | tf_op jit(solution)/shard_map/all_gather | solution.py:139
  380.8 42.4 %all-gather.16.cloned.1.call-done = bf16[256,2048]{1,0:T(8,128)(2,1)} async-done(((bf16[32,2048]{1,0:T(8,128)(2,1)}), bf16[256,2048]{1,0:T(8,128)(2,1)}) %all-gather.16.cloned.1.call-update) | async-done | bytes 1048592 | tf_op jit(solution)/shard_map/all_gather | solution.py:140
  423.2 9.2 %convolution_convert_fusion = bf16[1024,2048]{1,0:T(8,128)(2,1)} fusion(bf16[256,2048]{1,0:T(8,128)(2,1)} %all-gather.16.cloned.1.call-done, bf16[1024,2048]{1,0:T(8,128)(2,1)} %all-gather.10.cloned.1.call-done, bf16[256,2048]{1,0:T(8,128)(2,1)} %all-gather.14.cloned.1.call-done, f32[1024,256]{1,0:T(8,128)S(1)} %fusion.87), kind=kOutput, calls=%fused_computation.30 | convolution fusion | flops 2151153664 | bytes 11534336 | tf_op jit(solution)/shard_map/dot_general | solution.py:148
  432.6 1.1 constant_dynamic-slice_fusion
  434.1 0.7 maximum_bitcast_fusion.2
  434.9 98.5 %reduce-scatter.5.cloned.1.call-done = bf16[32,2048]{1,0:T(8,128)(2,1)} async-done(((bf16[1024,2048]{1,0:T(8,128)(2,1)}), bf16[32,2048]{1,0:T(8,128)(2,1)}) %reduce-scatter.5.cloned.1.call-update) | async-done | bytes 131088 | tf_op jit(solution)/shard_map/reduce_scatter | solution.py:147
  533.4 1.6 fusion.69
  (94 shorter events, 4.7 us)
Async XLA Ops:
  8.0 158.7 %copy-start = (bf16[64,2048]{1,0:T(8,128)(2,1)S(1)}, bf16[64,2048]{1,0:T(8,128)(2,1)}, u32[]{:S(2)}) copy-start(bf16[64,2048]{1,0:T(8,128)(2,1)} %param.18) | copy-start | bytes 786436
  8.0 69.8 %copy-start.10 = (f32[2048]{0:T(1024)S(1)}, f32[2048]{0:T(1024)}, u32[]{:S(2)}) copy-start(f32[2048]{0:T(1024)} %param.15) | copy-start | bytes 24580
  8.0 69.8 %copy-start.9 = (bf16[32,2048]{1,0:T(8,128)(2,1)S(1)}, bf16[32,2048]{1,0:T(8,128)(2,1)}, u32[]{:S(2)}) copy-start(bf16[32,2048]{1,0:T(8,128)(2,1)} %param.17) | copy-start | bytes 393220
  8.0 66.6 %all-gather.18.cloned.1.call-start = ((), (), s32[]{:S(2)}) async-start(), calls=%async_computation.10 | async-start | bytes 4325376 | tf_op jit(solution)/shard_map/all_gather | solution.py:78
  8.8 139.5 %all-gather.8.cloned.1.call-start = ((), (), s32[]{:S(2)}) async-start(), calls=%async_computation.3 | async-start | bytes 2162688 | tf_op jit(solution)/shard_map/all_gather | solution.py:82
  74.6 3.4 copy-start.2
  78.1 2.1 copy-start.5
  80.1 9.5 %copy-start.8 = (bf16[64,2048]{1,0:T(8,128)(2,1)S(1)}, bf16[64,2048]{1,0:T(8,128)(2,1)}, u32[]{:S(2)}) copy-start(bf16[64,2048]{1,0:T(8,128)(2,1)} %param.16) | copy-start | bytes 786436
  82.2 67.9 %all-to-all-start = ((bf16[8,16,32,128]{3,1,0,2:T(8,128)(2,1)}), bf16[8,16,32,128]{3,1,0,2:T(8,128)(2,1)S(1)}, u32[]{:S(2)}, u32[]{:S(2)}) async-start(bf16[8,16,32,128]{3,1,0,2:T(8,128)(2,1)} %select_bitcast_fusion), calls=%async_computation | async-start | bytes 2097152 | tf_op jit(solution)/shard_map/all_to_all | solution.py:104
  88.8 192.9 %reduce-scatter.3.cloned.1.call-start = ((), (), s32[]{:S(2)}) async-start(), calls=%async_computation.4 | async-start | bytes 4325376 | tf_op jit(solution)/shard_map/reduce_scatter | solution.py:129
  89.6 60.5 %copy-start.7 = (s32[1,256]{1,0:T(1,128)S(1)}, s32[1,256]{1,0:T(1,128)}, u32[]{:S(2)}) copy-start(s32[1,256]{1,0:T(1,128)} %param.24) | copy-start | bytes 3076
  164.3 2.0 copy-start.1
  172.6 109.1 %copy-start.3 = (bf16[1,32,2048]{2,1,0:T(8,128)(2,1)S(1)}, bf16[1,32,2048]{2,1,0:T(8,128)(2,1)}, u32[]{:S(2)}) copy-start(bf16[1,32,2048]{2,1,0:T(8,128)(2,1)} %param.14) | copy-start | bytes 393220
  172.6 110.2 %copy-start.6 = (f32[2048]{0:T(1024)S(1)}, f32[2048]{0:T(1024)}, u32[]{:S(2)}) copy-start(f32[2048]{0:T(1024)} %param.19) | copy-start | bytes 24580
  172.6 113.4 %all-gather.12.cloned.1.call-start = ((), (), s32[]{:S(2)}) async-start(), calls=%async_computation.6 | async-start | bytes 1179648 | tf_op jit(solution)/shard_map/all_gather | solution.py:138
  173.2 168.9 %all-gather.10.cloned.1.call-start = ((), (), s32[]{:S(2)}) async-start(), calls=%async_computation.5 | async-start | bytes 4325376 | tf_op jit(solution)/shard_map/all_gather | solution.py:136
  284.4 96.3 %all-gather.14.cloned.1.call-start = ((), (), s32[]{:S(2)}) async-start(), calls=%async_computation.7 | async-start | bytes 1179648 | tf_op jit(solution)/shard_map/all_gather | solution.py:139
  285.0 138.1 %all-gather.16.cloned.1.call-start = ((), (), s32[]{:S(2)}) async-start(), calls=%async_computation.8 | async-start | bytes 1179648 | tf_op jit(solution)/shard_map/all_gather | solution.py:140
  285.8 247.6 %reduce-scatter.5.cloned.1.call-start = ((), (), s32[]{:S(2)}) async-start(), calls=%async_computation.9 | async-start | bytes 4325376 | tf_op jit(solution)/shard_map/reduce_scatter | solution.py:147
  432.3 101.1 %copy-start.4 = (bf16[32,2048]{1,0:T(8,128)(2,1)S(1)}, bf16[32,2048]{1,0:T(8,128)(2,1)}, u32[]{:S(2)}) copy-start(bf16[32,2048]{1,0:T(8,128)(2,1)} %reduce-scatter.3.cloned.1.call-done) | copy-start | bytes 393220
Sparse Core Ops, SparseCore 0:
  11.4 63.1 all-gather.17
  80.3 67.9 all-gather.7
  172.7 108.9 reduce-scatter.2
Sparse Core Ops, SparseCore 1:
  174.9 48.2 all-gather.11
  284.5 57.5 all-gather.9
  343.8 37.0 all-gather.13
  382.6 40.5 all-gather.15
  432.5 100.9 reduce-scatter.4
where the time goes:
time: 543 us; the launch traced here: 542 us
  waiting for transfers between devices  464 us (85%)
  matrix products  29.7 us (5%)
  between operations  16.5 us (3%)
  other arithmetic  16.4 us (3%)
  local copies, waits for them, and re-layouts  8.66 us (2%)
  starting transfers between devices  7.14 us (1%)
    reduce_scatter x1, waiting for transfers between devices, on_device(): lax.psum_scatter(jnp.dot(rows_in, out_weight, preferred_element_type=jnp....  108 us
    reduce_scatter x1, waiting for transfers between devices, on_device(): lax.psum_scatter(jnp.dot(activated, down_rows, preferred_element_type=jnp...  98.5 us
    all_gather x1, waiting for transfers between devices, on_device(): all_tokens = lax.all_gather(own_tokens, 'dev', axis=0, tiled=True)  65.8 us
    all_gather x1, waiting for transfers between devices, on_device(): lax.all_gather(root_norm(residual, feedforward_gain), 'dev', axis=0, tile...  56.1 us
    all_gather x1, waiting for transfers between devices, on_device(): keyval_all = lax.all_gather(raw_columns, 'dev', axis=0, tiled=True)  55 us
    all_gather x1, waiting for transfers between devices, on_device(): lax.all_gather(down_weight, 'req', axis=0, tiled=True)  42.4 us
    all_gather x1, waiting for transfers between devices, on_device(): lax.all_gather(up_weight, 'req', axis=0, tiled=True)  34.9 us
    dot_general x8, matrix products, transposed_product(): lax.dot_general(left, right, (((1,), (1,)), ((), ())), preferred_element_...  12.1 us
  transfers between devices with their start and end apart: 9, of which 7 were waited for; matrix products, arithmetic and copies ran while one was open for 3% of the time, Pallas kernels for 0%

commit v1 on v0

--- a/solution.py
+++ b/solution.py
@@ -75,7 +75,9 @@
     member = lax.axis_index("dev")
     length = prefix_length[0]
     own_tokens = hidden_in[0]
-    all_tokens = lax.all_gather(own_tokens, "dev", axis=0, tiled=True)
+    all_tokens = jnp.concatenate(
+        lax.all_to_all(jnp.stack([own_tokens] * lax.axis_size("dev")), "dev", 0, 0), axis=0
+    )
     normed = root_norm(all_tokens, attention_gain)
     positions = length + jnp.arange(all_count, dtype=jnp.int32)
     raw_columns = transposed_product(keyval_weight, normed).astype(jnp.bfloat16)

time: 543 us -> 582 us (1.072)
  blocking collectives: 0 us -> 107 us
  waiting for transfers between devices: 464 us -> 391 us
    all_to_all x0 -> x1, blocking collectives: none -> 107 us  [on_device(): lax.all_to_all(jnp.stack([own_tokens] * lax.axis_size('dev')), 'dev', 0, 0)]
    all_gather x1 -> x0, waiting for transfers between devices: 65.8 us -> none  [on_device(): all_tokens = lax.all_gather(own_tokens, 'dev', axis=0, tiled=True)]
    all_gather x1, waiting for transfers between devices: 55 us -> 48.2 us  [on_device(): keyval_all = lax.all_gather(raw_columns, 'dev', axis=0, tiled=True)]
  transfers between devices with their start and end apart: 9 -> 8, of which waited for: 7 -> 6; matrix products, arithmetic and copies ran while one was open for 3% -> 3% of each run, Pallas kernels for 0% -> 0%
where the time goes in v1:
time: 582 us
  waiting for transfers between devices  391 us (67%)
  blocking collectives  107 us (18%)
  matrix products  29.5 us (5%)
  other arithmetic  17.4 us (3%)
  between operations  16.5 us (3%)
  local copies, waits for them, and re-layouts  13.9 us (2%)
    reduce_scatter x1, waiting for transfers between devices, on_device(): lax.psum_scatter(jnp.dot(rows_in, out_weight, preferred_element_type=jnp....  109 us
    all_to_all x1, blocking collectives, on_device(): lax.all_to_all(jnp.stack([own_tokens] * lax.axis_size('dev')), 'dev', 0, 0)  107 us
    reduce_scatter x1, waiting for transfers between devices, on_device(): lax.psum_scatter(jnp.dot(activated, down_rows, preferred_element_type=jnp...  99 us
    all_gather x1, waiting for transfers between devices, on_device(): lax.all_gather(root_norm(residual, feedforward_gain), 'dev', axis=0, tile...  56 us
    all_gather x1, waiting for transfers between devices, on_device(): keyval_all = lax.all_gather(raw_columns, 'dev', axis=0, tiled=True)  48.2 us
    all_gather x1, waiting for transfers between devices, on_device(): lax.all_gather(down_weight, 'req', axis=0, tiled=True)  42.4 us
    all_gather x1, waiting for transfers between devices, on_device(): lax.all_gather(up_weight, 'req', axis=0, tiled=True)  34.9 us
    dot_general x8, matrix products, transposed_product(): lax.dot_general(left, right, (((1,), (1,)), ((), ())), preferred_element_...  12 us
  transfers between devices with their start and end apart: 8, of which 6 were waited for; matrix products, arithmetic and copies ran while one was open for 3% of the time, Pallas kernels for 0%

profile of v1, /device:TPU:8, one launch (start us, length us, event | category | flops | bytes accessed | tf_op | source)
XLA Modules:
  0.0 581.7 jit_solution(6139534310196829828)
XLA Ops:
  8.1 1.5 stack.3
  9.5 107.5 %all_to_all.20 = bf16[32,32,2048]{2,1,0:T(8,128)(2,1)S(1)} all-to-all(bf16[32,32,2048]{2,1,0:T(8,128)(2,1)S(1)} %stack.3), channel_id=1, replica_groups=mesh['req'=8,'dev'=32] {'dev'}, dimensions={0} | all-to-all | bytes 8388608 | tf_op jit(solution)/shard_map/all_to_all | solution.py:79
  117.0 1.9 copy-done.2
  118.9 0.9 multiply_reduce_fusion
  119.9 3.3 fusion.12
  123.2 2.0 copy-done.1
  125.2 2.0 fusion.23
  127.3 0.8 gather_fusion.1
  128.1 1.1 select_bitcast_fusion
  129.3 5.1 all-to-all-start
  135.1 3.6 convolution_bitcast_fusion
  138.8 48.2 %all-gather.6.cloned.1.call-done = bf16[1024,1024]{1,0:T(8,128)(2,1)} async-done(((bf16[32,1024]{1,0:T(8,128)(2,1)}), bf16[1024,1024]{1,0:T(8,128)(2,1)}) %all-gather.6.cloned.1.call-update) | async-done | bytes 2097168 | tf_op jit(solution)/shard_map/all_gather | solution.py:84
  187.0 1.0 dynamic-slice_bitcast_fusion
  188.0 0.6 fusion.53
  188.9 13.4 %while.14 = (s32[]{:T(128)}, f32[1024]{0:T(1024)S(1)}, f32[1024]{0:T(1024)S(1)}, f32[1024,64]{0,1:T(8,128)S(1)}, s32[]{:T(128)}, /*index=5*/s32[]{:T(128)}, s32[...) while((s32[]{:T(128)}, f32[1024]{0:T(1024)S(1)}, ...), condition=%wide.region_4.5_spmd, body=%wide.region_1.4_spmd.sunk | while | flops 139661504 | bytes 7807755 | solution.py:125
  189.0 0.6 gather_fusion
  189.9 0.7 add_compare_fusion.2
  191.0 0.5 fusion.94
  191.5 0.6 convolution_add_fusion.2
  192.3 0.6 gather_fusion
  193.2 0.7 add_compare_fusion.2
  194.3 0.5 fusion.94
  194.9 0.6 convolution_add_fusion.2
  195.6 0.6 gather_fusion
  196.6 0.7 add_compare_fusion.2
  197.7 0.5 fusion.94
  198.2 0.6 convolution_add_fusion.2
  199.0 0.6 gather_fusion
  199.9 0.7 add_compare_fusion.2
  201.5 0.6 convolution_add_fusion.2
  202.2 0.8 fusion.14
  203.0 2.0 copy-done.3
  205.5 5.8 convolution_convert_fusion.1
  211.4 0.5 all-gather.10.cloned.1.call-update
  211.9 108.7 %reduce-scatter.3.cloned.1.call-done = bf16[32,2048]{1,0:T(8,128)(2,1)} async-done(((bf16[1024,2048]{1,0:T(8,128)(2,1)}), bf16[32,2048]{1,0:T(8,128)(2,1)}) %reduce-scatter.3.cloned.1.call-update) | async-done | bytes 131088 | tf_op jit(solution)/shard_map/reduce_scatter | solution.py:131
  320.7 1.1 multiply_reduce_fusion.1
  321.7 1.7 multiply_convert_fusion
  323.5 0.5 all-gather.12.cloned.1.call-update
  324.0 0.7 all-gather.14.cloned.1.call-update
  325.0 56.0 %all-gather.8.cloned.1.call-done = bf16[1024,2048]{1,0:T(8,128)(2,1)} async-done(((bf16[32,2048]{1,0:T(8,128)(2,1)}), bf16[1024,2048]{1,0:T(8,128)(2,1)}) %all-gather.8.cloned.1.call-update) | async-done | bytes 4194320 | tf_op jit(solution)/shard_map/all_gather | solution.py:138
  381.0 3.8 fusion.74
  384.8 34.9 %all-gather.12.cloned.1.call-done = bf16[256,2048]{1,0:T(8,128)(2,1)} async-done(((bf16[32,2048]{1,0:T(8,128)(2,1)}), bf16[256,2048]{1,0:T(8,128)(2,1)}) %all-gather.12.cloned.1.call-update) | async-done | bytes 1048592 | tf_op jit(solution)/shard_map/all_gather | solution.py:141
  419.7 42.4 %all-gather.14.cloned.1.call-done = bf16[256,2048]{1,0:T(8,128)(2,1)} async-done(((bf16[32,2048]{1,0:T(8,128)(2,1)}), bf16[256,2048]{1,0:T(8,128)(2,1)}) %all-gather.14.cloned.1.call-update) | async-done | bytes 1048592 | tf_op jit(solution)/shard_map/all_gather | solution.py:142
  462.1 9.2 %convolution_convert_fusion = bf16[1024,2048]{1,0:T(8,128)(2,1)} fusion(bf16[256,2048]{1,0:T(8,128)(2,1)} %all-gather.14.cloned.1.call-done, bf16[1024,2048]{1,0:T(8,128)(2,1)} %all-gather.8.cloned.1.call-done, bf16[256,2048]{1,0:T(8,128)(2,1)} %all-gather.12.cloned.1.call-done, f32[1024,256]{1,0:T(8,128)S(1)} %fusion.74), kind=kOutput, calls=%fused_computation.29 | convolution fusion | flops 2151153664 | bytes 11534336 | tf_op jit(solution)/shard_map/dot_general | solution.py:150
  471.5 1.1 constant_dynamic-slice_fusion
  473.0 0.7 maximum_bitcast_fusion.2
  473.8 99.0 %reduce-scatter.5.cloned.1.call-done = bf16[32,2048]{1,0:T(8,128)(2,1)} async-done(((bf16[1024,2048]{1,0:T(8,128)(2,1)}), bf16[32,2048]{1,0:T(8,128)(2,1)}) %reduce-scatter.5.cloned.1.call-update) | async-done | bytes 131088 | tf_op jit(solution)/shard_map/reduce_scatter | solution.py:149
  572.8 1.6 fusion.56
  (97 shorter events, 6.0 us)
Async XLA Ops:
  8.0 197.5 %copy-start = (bf16[64,2048]{1,0:T(8,128)(2,1)S(1)}, bf16[64,2048]{1,0:T(8,128)(2,1)}, u32[]{:S(2)}) copy-start(bf16[64,2048]{1,0:T(8,128)(2,1)} %param.18) | copy-start | bytes 786436
  8.0 179.0 %all-gather.6.cloned.1.call-start = ((), (), s32[]{:S(2)}) async-start(), calls=%async_computation.4 | async-start | bytes 2162688 | tf_op jit(solution)/shard_map/all_gather | solution.py:84
  117.0 1.9 copy-start.2
  118.9 1.0 copy-start.9
  119.9 5.3 copy-start.8
  123.2 2.0 copy-start.1
  125.2 2.0 copy-start.7
  127.2 7.9 %copy-start.6 = (bf16[64,2048]{1,0:T(8,128)(2,1)S(1)}, bf16[64,2048]{1,0:T(8,128)(2,1)}, u32[]{:S(2)}) copy-start(bf16[64,2048]{1,0:T(8,128)(2,1)} %param.16) | copy-start | bytes 786436
  129.3 59.5 %all-to-all-start = ((bf16[8,16,32,128]{3,1,0,2:T(8,128)(2,1)}), bf16[8,16,32,128]{3,1,0,2:T(8,128)(2,1)S(1)}, u32[]{:S(2)}, u32[]{:S(2)}) async-start(bf16[8,16,32,128]{3,1,0,2:T(8,128)(2,1)} %select_bitcast_fusion), calls=%async_computation | async-start | bytes 2097152 | tf_op jit(solution)/shard_map/all_to_all | solution.py:106
  134.3 186.3 %reduce-scatter.3.cloned.1.call-start = ((), (), s32[]{:S(2)}) async-start(), calls=%async_computation.5 | async-start | bytes 4325376 | tf_op jit(solution)/shard_map/reduce_scatter | solution.py:131
  135.1 53.7 %copy-start.11 = (s32[1,256]{1,0:T(1,128)S(1)}, s32[1,256]{1,0:T(1,128)}, u32[]{:S(2)}) copy-start(s32[1,256]{1,0:T(1,128)} %param.24) | copy-start | bytes 3076
  203.0 2.0 copy-start.3
  211.3 109.4 %copy-start.4 = (bf16[1,32,2048]{2,1,0:T(8,128)(2,1)S(1)}, bf16[1,32,2048]{2,1,0:T(8,128)(2,1)}, u32[]{:S(2)}) copy-start(bf16[1,32,2048]{2,1,0:T(8,128)(2,1)} %param.14) | copy-start | bytes 393220
  211.3 110.5 %copy-start.10 = (f32[2048]{0:T(1024)S(1)}, f32[2048]{0:T(1024)}, u32[]{:S(2)}) copy-start(f32[2048]{0:T(1024)} %param.19) | copy-start | bytes 24580
  211.3 113.7 %all-gather.10.cloned.1.call-start = ((), (), s32[]{:S(2)}) async-start(), calls=%async_computation.7 | async-start | bytes 1179648 | tf_op jit(solution)/shard_map/all_gather | solution.py:140
  211.9 169.1 %all-gather.8.cloned.1.call-start = ((), (), s32[]{:S(2)}) async-start(), calls=%async_computation.6 | async-start | bytes 4325376 | tf_op jit(solution)/shard_map/all_gather | solution.py:138
  323.4 96.3 %all-gather.12.cloned.1.call-start = ((), (), s32[]{:S(2)}) async-start(), calls=%async_computation.8 | async-start | bytes 1179648 | tf_op jit(solution)/shard_map/all_gather | solution.py:141
  324.0 138.1 %all-gather.14.cloned.1.call-start = ((), (), s32[]{:S(2)}) async-start(), calls=%async_computation.9 | async-start | bytes 1179648 | tf_op jit(solution)/shard_map/all_gather | solution.py:142
  324.7 248.0 %reduce-scatter.5.cloned.1.call-start = ((), (), s32[]{:S(2)}) async-start(), calls=%async_computation.10 | async-start | bytes 4325376 | tf_op jit(solution)/shard_map/reduce_scatter | solution.py:149
  471.3 101.5 %copy-start.5 = (bf16[32,2048]{1,0:T(8,128)(2,1)S(1)}, bf16[32,2048]{1,0:T(8,128)(2,1)}, u32[]{:S(2)}) copy-start(bf16[32,2048]{1,0:T(8,128)(2,1)} %reduce-scatter.3.cloned.1.call-done) | copy-start | bytes 393220
Sparse Core Ops, SparseCore 0:
  127.3 59.6 all-gather.5
  211.4 109.1 reduce-scatter.2
  471.4 101.2 reduce-scatter.4
Sparse Core Ops, SparseCore 1:
  213.6 48.3 all-gather.9
  323.5 57.5 all-gather.7
  382.7 37.0 all-gather.11
  421.5 40.5 all-gather.13
